TPU v7x, 32 devices: a whole 2x2x4 slice. The times are simulated.
32 devices in a mesh: row: 8 (over z, y), col: 4 (over x, core).
Axes of the slice: x: 2, y: 2, z: 4, core: 2. Of those that a mesh axis runs over, the one named last changes fastest.
Arguments:
- inputs: bfloat16 [768, 8192], P('row', 'col'), may hold values from -16 to 16
- norm_gain: float32 [8192], P('col'), may hold values from 0.25 to 4
- w_gate: bfloat16 [8192, 28672], P('col', 'row'), may hold values from -0.09375 to 0.09375
- w_up: bfloat16 [8192, 28672], P('col', 'row'), may hold values from -0.09375 to 0.09375
- w_down: bfloat16 [28672, 8192], P('row', 'col'), may hold values from -0.050111483 to 0.050111483
- mask_gate: int32 [128, 448], P('col', 'row'), may hold values 0 or 1
- mask_up: int32 [128, 448], P('col', 'row'), may hold values 0 or 1
- mask_down: int32 [448, 128], P('row', 'col'), may hold values 0 or 1
- grad_out: bfloat16 [768, 8192], P('row', 'col'), may hold values from -5 to 5
Outputs:
- output: bfloat16 [768, 8192], P('row', 'col')
- grad_inputs: bfloat16 [768, 8192], P('row', 'col')
- grad_gain: float32 [8192], P('col')
- grad_w_gate: bfloat16 [8192, 28672], P('col', 'row')
- grad_w_up: bfloat16 [8192, 28672], P('col', 'row')
- grad_w_down: bfloat16 [28672, 8192], P('row', 'col')
All inputs are finite; a program needn't handle non-finite values. No bound on the sum of `mask_gate` or of `mask_up` or of `mask_down` on one device may be relied on, other than what follows from the above.
Results may differ from a plain program's by a relative error of at most 0.02.
Values may be sent and summed in bfloat16 or wider, within the bound.
No kernel may reach another device: no remote copies, remote signals or barrier semaphores. Data moves between devices by JAX's collectives and lax.ppermute only.
A program may use at most 256 MiB of HBM per device.

v0:
```python
import jax
import jax.numpy as jnp
from jax import lax
from jax.sharding import PartitionSpec as P

D = 8192
BLOCK = 64
epsilon = 1e-05


def expand_mask(weight, block_mask):
    mask_rows, mask_cols = block_mask.shape
    blocked = (
        weight.reshape(mask_rows, BLOCK, mask_cols, BLOCK)
        * block_mask.astype(jnp.bfloat16)[:, None, :, None]
    )
    return blocked.reshape(weight.shape)


def contract_rows(left, right):
    return lax.dot_general(
        left, right, (((0,), (0,)), ((), ())), preferred_element_type=jnp.float32
    )


def contract_cols(left, right):
    return lax.dot_general(
        left, right, (((1,), (1,)), ((), ())), preferred_element_type=jnp.float32
    )


def shards(inputs, norm_gain, w_gate, w_up, w_down, mask_gate, mask_up, mask_down, grad_out):
    gate_eff = expand_mask(w_gate, mask_gate)
    up_eff = expand_mask(w_up, mask_up)
    down_eff = expand_mask(w_down, mask_down)
    local_rows = inputs.shape[0]
    inputs_all, grads_all = (
        lax.all_gather(inputs, "row", axis=0, tiled=True),
        lax.all_gather(grad_out, "row", axis=0, tiled=True),
    )
    ff_width = w_gate.shape[1]
    inputs_wide = inputs_all.astype(jnp.float32)
    squares = lax.psum(jnp.sum(inputs_wide * inputs_wide, axis=1, keepdims=True), "col")
    inv_rms = lax.rsqrt(squares / D + epsilon)
    normed = inputs_wide * inv_rms
    hidden_in = (normed * norm_gain).astype(jnp.bfloat16)
    row_block = hidden_in
    projected = lax.psum_scatter(
        jnp.concatenate(
            [
                jnp.dot(row_block, gate_eff, preferred_element_type=jnp.float32),
                jnp.dot(row_block, up_eff, preferred_element_type=jnp.float32),
            ],
            axis=1,
        ).astype(jnp.bfloat16),
        "col",
        scatter_dimension=0,
        tiled=True,
    ).astype(jnp.float32)
    gate_value = projected[:, :ff_width]
    up_value = projected[:, ff_width:]
    sigmoid_gate = jax.nn.sigmoid(gate_value)
    silu_gate = gate_value * sigmoid_gate
    hidden = (silu_gate * up_value).astype(jnp.bfloat16)
    hidden_all = lax.all_gather(hidden, "col", axis=0, tiled=True)
    row_block = hidden_all
    mixed_out = lax.psum_scatter(
        jnp.dot(row_block, down_eff, preferred_element_type=jnp.float32).astype(jnp.bfloat16),
        "row",
        scatter_dimension=0,
        tiled=True,
    ).astype(jnp.float32)
    output = (inputs.astype(jnp.float32) + mixed_out).astype(jnp.bfloat16)
    grad_w_down = expand_mask(contract_rows(hidden_all, grads_all).astype(jnp.bfloat16), mask_down)
    row_block = grads_all
    d_hidden = lax.psum_scatter(
        contract_cols(row_block, down_eff).astype(jnp.bfloat16),
        "col",
        scatter_dimension=0,
        tiled=True,
    ).astype(jnp.float32)
    d_up = (d_hidden * silu_gate).astype(jnp.bfloat16)
    d_gate = (
        d_hidden * up_value * sigmoid_gate * (1.0 + gate_value * (1.0 - sigmoid_gate))
    ).astype(jnp.bfloat16)
    d_gate_all, d_up_all = (
        lax.all_gather(d_gate, "col", axis=0, tiled=True),
        lax.all_gather(d_up, "col", axis=0, tiled=True),
    )
    grad_w_gate = expand_mask(contract_rows(hidden_in, d_gate_all).astype(jnp.bfloat16), mask_gate)
    grad_w_up = expand_mask(contract_rows(hidden_in, d_up_all).astype(jnp.bfloat16), mask_up)
    d_norm_in = lax.psum_scatter(
        (contract_cols(d_gate_all, gate_eff) + contract_cols(d_up_all, up_eff)).astype(
            jnp.bfloat16
        ),
        "row",
        scatter_dimension=0,
        tiled=True,
    ).astype(jnp.float32)
    row_start = lax.axis_index("row") * local_rows
    normed_local = lax.dynamic_slice_in_dim(normed, row_start, local_rows, 0)
    inv_rms_local = lax.dynamic_slice_in_dim(inv_rms, row_start, local_rows, 0)
    gain_part = jnp.sum(d_norm_in * normed_local, axis=0)
    d_normed = d_norm_in * norm_gain
    inner_part = jnp.sum(d_normed * normed_local, axis=1, keepdims=True)
    row_inner = lax.psum(inner_part, "col") / D
    grad_gain = lax.psum(gain_part, "row")
    grad_inputs = (
        grad_out.astype(jnp.float32) + inv_rms_local * (d_normed - normed_local * row_inner)
    ).astype(jnp.bfloat16)
    return (output, grad_inputs, grad_gain, grad_w_gate, grad_w_up, grad_w_down)


def solution(mesh):
    in_specs = (
        P("row", "col"),
        P("col"),
        P("col", "row"),
        P("col", "row"),
        P("row", "col"),
        P("col", "row"),
        P("col", "row"),
        P("row", "col"),
        P("row", "col"),
    )
    out_specs = (
        P("row", "col"),
        P("row", "col"),
        P("col"),
        P("col", "row"),
        P("col", "row"),
        P("row", "col"),
    )
    return jax.shard_map(shards, mesh=mesh, in_specs=in_specs, out_specs=out_specs, check_vma=False)
```

profile of v0, /device:TPU:0, one launch (start us, length us, event | category | flops | bytes accessed | tf_op | source)
XLA Modules:
  0.0 632.4 jit_solution(2924886407965607107)
XLA Ops:
  7.2 0.0 all-gather.6.cloned.1.call-start
  7.2 0.7 all-gather.6.cloned.1.call-update
  7.9 0.0 all-gather.10.cloned.1.call-start
  7.9 0.7 all-gather.10.cloned.1.call-update
  8.6 0.0 reduce-scatter.5.cloned.1.call-start
  8.7 0.7 convert_element_type.77
  9.4 10.0 %mul.142 = bf16[32,64,56,64]{3,2,1,0:T(8,128)(2,1)} broadcast(bf16[32,56]{1,0:T(8,128)(2,1)S(1)} %convert_element_type.77), dimensions={0,2} | broadcast | bytes 14683648 | tf_op jit(solution)/shard_map/mul | solution.py:14
  19.4 36.2 %mul.143 = bf16[2048,3584]{1,0:T(8,128)(2,1)} reshape(bf16[32,64,56,64]{3,2,1,0:T(8,128)(2,1)} %mul.142) | data formatting | bytes 29360128 | tf_op jit(solution)/shard_map/mul | solution.py:14
  55.7 10.1 %mul.139 = bf16[32,64,56,64]{3,2,1,0:T(8,128)(2,1)} broadcast(bf16[32,56]{1,0:T(8,128)(2,1)S(1)} %convert_element_type.76), dimensions={0,2} | broadcast | bytes 14683648 | tf_op jit(solution)/shard_map/mul | solution.py:14
  65.8 36.3 %mul.140 = bf16[2048,3584]{1,0:T(8,128)(2,1)} reshape(bf16[32,64,56,64]{3,2,1,0:T(8,128)(2,1)} %mul.139) | data formatting | bytes 29360128 | tf_op jit(solution)/shard_map/mul | solution.py:14
  102.1 18.6 %mul.144 = bf16[2048,3584]{1,0:T(8,128)(2,1)} multiply(bf16[2048,3584]{1,0:T(8,128)(2,1)} %param.12, bf16[2048,3584]{1,0:T(8,128)(2,1)} %mul.143) | non-fusion elementwise | flops 7340032 | bytes 44040192 | tf_op jit(solution)/shard_map/mul | solution.py:14
  120.7 1.1 copy-done
  121.8 14.7 %mul.141 = bf16[2048,3584]{1,0:T(8,128)(2,1)} multiply(bf16[2048,3584]{1,0:T(8,128)(2,1)} %param.11, bf16[2048,3584]{1,0:T(8,128)(2,1)S(1)} %copy-done) | non-fusion elementwise | flops 7340032 | bytes 44040192 | tf_op jit(solution)/shard_map/mul | solution.py:14
  136.6 2.7 fusion.3
  139.3 8.2 %psum.21 = f32[768,1]{0,1:T(1,128)S(1)} all-reduce(f32[768,1]{0,1:T(1,128)S(1)} %broadcast_in_dim.4), channel_id=1, replica_groups=mesh['row'=8,'col'=4] {'col'}, use_global_device_ids=true, to_apply=%region_1.0 | all-reduce | flops 768 | bytes 6144 | tf_op jit(solution)/shard_map/psum | solution.py:43
  147.5 0.6 fusion.23
  148.1 0.0 copy-done.5
  148.1 0.0 copy-start.1
  148.1 17.5 %convolution_convert_fusion.4 = bf16[768,3584]{1,0:T(8,128)(2,1)} fusion(bf16[2048,3584]{1,0:T(8,128)(2,1)} %mul.144, f32[2048]{0:T(1024)S(1)} %copy-done.5, f32[768]{0:T(1024)S(1)} %get-tuple-element.8, bf16[768,2048]{1,0:T(8,128)(2,1)} %all-gather.6.cloned.1.call-done), kind=kOutput, calls=%fused_computation.10 | convolution fusion | flops 11283333120 | bytes 23342080 | tf_op jit(solution)/shard_map/dot_general | solution.py:52
  165.6 0.0 slice-done
  165.6 13.5 %convolution_convert_fusion.5 = bf16[768,3584]{1,0:T(8,128)(2,1)} fusion(bf16[2048,3584]{1,0:T(8,128)(2,1)S(1)} %bitcast.26, f32[2048]{0:T(1024)S(1)} %copy-done.5, f32[768]{0:T(1024)S(1)} %get-tuple-element.8, bf16[768,2048]{1,0:T(8,128)(2,1)S(1)} %copy-done.1), kind=kOutput, calls=%fused_computation.11 | convolution fusion | flops 11283333120 | bytes 23342080 | tf_op jit(solution)/shard_map/dot_general | solution.py:51
  179.1 9.5 %pad_maximum_fusion = bf16[768,7168]{1,0:T(8,128)(2,1)} fusion(bf16[768,3584]{1,0:T(8,128)(2,1)} %convolution_convert_fusion.4, bf16[768,3584]{1,0:T(8,128)(2,1)} %convolution_convert_fusion.5), kind=kLoop, calls=%fused_computation.6 | loop fusion | flops 22020096 | bytes 22020096 | tf_op jit(solution)/shard_map/concatenate | solution.py:49
  188.6 0.0 reduce-scatter.5.cloned.1.call-update
  188.6 0.5 reduce-scatter.9.cloned.1.call-start
  189.1 0.2 copy-done.8
  189.3 0.1 copy.15
  189.4 14.1 %mul.147 = bf16[56,64,32,64]{3,2,1,0:T(8,128)(2,1)} broadcast(bf16[56,32]{1,0:T(8,128)(2,1)S(1)} %copy.15), dimensions={0,2} | broadcast | bytes 14683648 | tf_op jit(solution)/shard_map/mul | solution.py:14
  203.6 40.8 %mul.148 = bf16[3584,2048]{1,0:T(8,128)(2,1)} reshape(bf16[56,64,32,64]{3,2,1,0:T(8,128)(2,1)} %mul.147) | data formatting | bytes 29360128 | tf_op jit(solution)/shard_map/mul | solution.py:14
  244.4 19.8 %fusion.4 = bf16[768,3584]{1,0:T(8,128)(2,1)} fusion(bf16[768,2048]{1,0:T(8,128)(2,1)} %all-gather.10.cloned.1.call-done, bf16[3584,2048]{1,0:T(8,128)(2,1)} %param.13, bf16[3584,2048]{1,0:T(8,128)(2,1)} %mul.148), kind=kOutput, calls=%fused_computation.15 | convolution fusion | flops 11284381696 | bytes 38010880 | tf_op jit(solution)/shard_map/dot_general | solution.py:27
  264.1 0.0 reduce-scatter.9.cloned.1.call-update
  264.2 0.0 all-gather.12.cloned.1.call-start
  264.2 12.5 %reduce-scatter.5.cloned.1.call-done = bf16[192,7168]{1,0:T(8,128)(2,1)} async-done(((bf16[768,7168]{1,0:T(8,128)(2,1)}), bf16[192,7168]{1,0:T(8,128)(2,1)}) %reduce-scatter.5.cloned.1.call-update) | async-done | bytes 2752528 | tf_op jit(solution)/shard_map/reduce_scatter | solution.py:48
  276.7 4.8 convert_element_type.78
  281.5 50.6 %reduce-scatter.9.cloned.1.call-done = bf16[192,3584]{1,0:T(8,128)(2,1)} async-done(((bf16[768,3584]{1,0:T(8,128)(2,1)}), bf16[192,3584]{1,0:T(8,128)(2,1)}) %reduce-scatter.9.cloned.1.call-update) | async-done | bytes 1376272 | tf_op jit(solution)/shard_map/reduce_scatter | solution.py:76
  332.1 5.0 fusion.14
  337.1 0.0 all-gather.12.cloned.1.call-update
  337.1 0.0 all-gather.14.cloned.1.call-start
  337.2 0.5 all-gather.14.cloned.1.call-update
  337.7 0.0 all-gather.8.cloned.1.call-start
  337.8 0.7 all-gather.8.cloned.1.call-update
  338.5 0.0 reduce-scatter.11.cloned.1.call-start
  338.5 40.7 %all-gather.12.cloned.1.call-done = bf16[768,3584]{1,0:T(8,128)(2,1)} async-done(((bf16[192,3584]{1,0:T(8,128)(2,1)}), bf16[768,3584]{1,0:T(8,128)(2,1)}) %all-gather.12.cloned.1.call-update) | async-done | bytes 5505040 | tf_op jit(solution)/shard_map/all_gather | solution.py:87
  379.2 18.3 %fusion.24 = f32[768,2048]{1,0:T(8,128)} fusion(bf16[768,3584]{1,0:T(8,128)(2,1)} %all-gather.12.cloned.1.call-done, bf16[2048,3584]{1,0:T(8,128)(2,1)} %mul.141), kind=kOutput, calls=%fused_computation.43 | convolution fusion | flops 11274289152 | bytes 26476544 | tf_op jit(solution)/shard_map/dot_general | solution.py:27
  397.5 25.1 %all-gather.14.cloned.1.call-done = bf16[768,3584]{1,0:T(8,128)(2,1)} async-done(((bf16[192,3584]{1,0:T(8,128)(2,1)}), bf16[768,3584]{1,0:T(8,128)(2,1)}) %all-gather.14.cloned.1.call-update) | async-done | bytes 5505040 | tf_op jit(solution)/shard_map/all_gather | solution.py:88
  422.6 18.5 %add_convert_fusion = bf16[768,2048]{1,0:T(8,128)(2,1)} fusion(f32[768,2048]{1,0:T(8,128)} %fusion.24, bf16[768,3584]{1,0:T(8,128)(2,1)} %all-gather.14.cloned.1.call-done, bf16[2048,3584]{1,0:T(8,128)(2,1)} %mul.144), kind=kOutput, calls=%fused_computation.13 | convolution fusion | flops 11277434880 | bytes 29622272 | tf_op jit(solution)/shard_map/dot_general | solution.py:27
  441.1 0.0 reduce-scatter.11.cloned.1.call-update
  441.1 0.2 reduce-scatter.7.cloned.1.call-start
  441.4 0.8 dynamic-slice_bitcast_fusion
  442.1 0.0 copy-done.2
  442.1 3.1 convert_multiply_fusion
  445.2 20.8 %all-gather.8.cloned.1.call-done = bf16[768,3584]{1,0:T(8,128)(2,1)} async-done(((bf16[192,3584]{1,0:T(8,128)(2,1)}), bf16[768,3584]{1,0:T(8,128)(2,1)}) %all-gather.8.cloned.1.call-update) | async-done | bytes 5505040 | tf_op jit(solution)/shard_map/all_gather | solution.py:65
  466.0 19.7 %fusion.8 = bf16[768,2048]{1,0:T(8,128)(2,1)} fusion(bf16[768,3584]{1,0:T(8,128)(2,1)} %all-gather.8.cloned.1.call-done, bf16[3584,2048]{1,0:T(8,128)(2,1)} %param.13, bf16[3584,2048]{1,0:T(8,128)(2,1)} %mul.148), kind=kOutput, calls=%fused_computation.21 | convolution fusion | flops 11283202048 | bytes 38010880 | tf_op jit(solution)/shard_map/dot_general | solution.py:68
  485.7 0.0 reduce-scatter.7.cloned.1.call-update
  485.8 18.6 %fusion = bf16[2048,3584]{1,0:T(8,128)(2,1)} fusion(bf16[2048,3584]{1,0:T(8,128)(2,1)} %mul.140, bf16[768,3584]{1,0:T(8,128)(2,1)} %all-gather.12.cloned.1.call-done, f32[2048]{0:T(1024)S(1)} %copy-done.6, f32[768]{0:T(1024)S(1)} %get-tuple-element.8, bf16[768,2048]{1,0:T(8,128)(2,1)S(1)} %copy-done.2), kind=kOutput, calls=%fused_computation.3 | convolution fusion | flops 11295260672 | bytes 38022144 | tf_op jit(solution)/shard_map/dot_general | solution.py:21
  504.4 18.7 %fusion.1 = bf16[2048,3584]{1,0:T(8,128)(2,1)} fusion(bf16[2048,3584]{1,0:T(8,128)(2,1)} %mul.143, bf16[768,3584]{1,0:T(8,128)(2,1)} %all-gather.14.cloned.1.call-done, f32[2048]{0:T(1024)S(1)} %copy-done.6, f32[768]{0:T(1024)S(1)} %get-tuple-element.8, bf16[768,2048]{1,0:T(8,128)(2,1)S(1)} %copy-done.2), kind=kOutput, calls=%fused_computation.4 | convolution fusion | flops 11295260672 | bytes 38022144 | tf_op jit(solution)/shard_map/dot_general | solution.py:21
  523.1 20.3 %fusion.2 = bf16[3584,2048]{1,0:T(8,128)(2,1)} fusion(bf16[3584,2048]{1,0:T(8,128)(2,1)} %mul.148, bf16[768,3584]{1,0:T(8,128)(2,1)} %all-gather.8.cloned.1.call-done, bf16[768,2048]{1,0:T(8,128)(2,1)} %all-gather.10.cloned.1.call-done), kind=kOutput, calls=%fused_computation.5 | convolution fusion | flops 11288969216 | bytes 38010880 | tf_op jit(solution)/shard_map/dot_general | solution.py:21
  543.4 0.6 reduce-scatter.11.cloned.1.call-done
  544.0 1.5 fusion.22
  545.6 5.9 psum.22
  551.5 22.2 %psum.23 = f32[2048]{0:T(1024)} all-reduce(f32[2048]{0:T(1024)S(1)} %get-tuple-element.6), channel_id=1, replica_groups=mesh['row'=8,'col'=4] {'row'}, use_global_device_ids=true, to_apply=%region_9.0 | all-reduce | flops 2048 | bytes 16384 | tf_op jit(solution)/shard_map/psum | solution.py:107
  573.6 47.9 %reduce-scatter.7.cloned.1.call-done = bf16[96,2048]{1,0:T(8,128)(2,1)} async-done(((bf16[768,2048]{1,0:T(8,128)(2,1)}), bf16[96,2048]{1,0:T(8,128)(2,1)}) %reduce-scatter.7.cloned.1.call-update) | async-done | bytes 393232 | tf_op jit(solution)/shard_map/reduce_scatter | solution.py:67
  621.5 0.0 copy-done.3
  621.5 1.8 add_convert_fusion.1
  623.4 2.3 fusion.21
  (26 shorter events, 0.1 us)
Async XLA Ops:
  7.2 129.4 %all-gather.6.cloned.1.call-start = ((), (), s32[]{:S(2)}) async-start(), calls=%async_computation.4 | async-start | bytes 3538944 | tf_op jit(solution)/shard_map/all_gather | solution.py:38
  7.9 236.5 %all-gather.10.cloned.1.call-start = ((), (), s32[]{:S(2)}) async-start(), calls=%async_computation.8 | async-start | bytes 3538944 | tf_op jit(solution)/shard_map/all_gather | solution.py:39
  8.6 268.0 %reduce-scatter.5.cloned.1.call-start = ((), (), s32[]{:S(2)}) async-start(), calls=%async_computation.5 | async-start | bytes 13762560 | tf_op jit(solution)/shard_map/reduce_scatter | solution.py:48
  19.4 36.2 %copy-start.7 = (s32[32,56]{1,0:T(8,128)S(1)}, s32[32,56]{1,0:T(8,128)}, u32[]{:S(2)}) copy-start(s32[32,56]{1,0:T(8,128)} %param.14) | copy-start | bytes 21508
  102.1 19.7 %copy-start = (bf16[2048,3584]{1,0:T(8,128)(2,1)S(1)}, bf16[2048,3584]{1,0:T(8,128)(2,1)}, u32[]{:S(2)}) copy-start(bf16[2048,3584]{1,0:T(8,128)(2,1)} %mul.140) | copy-start | bytes 44040196
  121.8 26.2 %copy-start.5 = (f32[2048]{0:T(1024)S(1)}, f32[2048]{0:T(1024)}, u32[]{:S(2)}) copy-start(f32[2048]{0:T(1024)} %param.10) | copy-start | bytes 24580
  136.6 29.0 %slice-start = ((s8[14680064]{0:T(1024)(128)(4,1)}), s8[2097152]{0:T(1024)(128)(4,1)S(1)}, s32[]{:S(2)}) async-start(s8[14680064]{0:T(1024)(128)(4,1)} %bitcast.25), calls=%async_computation.13 | async-start | bytes 4194304
  148.1 17.5 %slice-start.1 = ((s8[14680064]{0:T(1024)(128)(4,1)}), s8[4194304]{0:T(1024)(128)(4,1)S(1)}, s32[]{:S(2)}) async-start(s8[14680064]{0:T(1024)(128)(4,1)} %bitcast.25), calls=%async_computation.14 | async-start | bytes 8388608
  148.1 17.5 %slice-start.2 = ((s8[14680064]{0:T(1024)(128)(4,1)}), s8[4194304]{0:T(1024)(128)(4,1)S(1)}, s32[]{:S(2)}) async-start(s8[14680064]{0:T(1024)(128)(4,1)} %bitcast.25), calls=%async_computation.15 | async-start | bytes 8388608
  148.1 17.5 %slice-start.3 = ((s8[14680064]{0:T(1024)(128)(4,1)}), s8[4194304]{0:T(1024)(128)(4,1)S(1)}, s32[]{:S(2)}) async-start(s8[14680064]{0:T(1024)(128)(4,1)} %bitcast.25), calls=%async_computation.16 | async-start | bytes 8388608
  148.1 17.5 %copy-start.1 = (bf16[768,2048]{1,0:T(8,128)(2,1)S(1)}, bf16[768,2048]{1,0:T(8,128)(2,1)}, u32[]{:S(2)}) copy-start(bf16[768,2048]{1,0:T(8,128)(2,1)} %all-gather.6.cloned.1.call-done) | copy-start | bytes 9437188
  188.6 0.7 copy-start.8
  188.6 143.5 %reduce-scatter.9.cloned.1.call-start = ((), (), s32[]{:S(2)}) async-start(), calls=%async_computation.9 | async-start | bytes 6881280 | tf_op jit(solution)/shard_map/reduce_scatter | solution.py:76
  264.2 115.1 %all-gather.12.cloned.1.call-start = ((), (), s32[]{:S(2)}) async-start(), calls=%async_computation.10 | async-start | bytes 6881280 | tf_op jit(solution)/shard_map/all_gather | solution.py:87
  337.1 85.4 %all-gather.14.cloned.1.call-start = ((), (), s32[]{:S(2)}) async-start(), calls=%async_computation.11 | async-start | bytes 6881280 | tf_op jit(solution)/shard_map/all_gather | solution.py:88
  337.7 128.3 %all-gather.8.cloned.1.call-start = ((), (), s32[]{:S(2)}) async-start(), calls=%async_computation.6 | async-start | bytes 6881280 | tf_op jit(solution)/shard_map/all_gather | solution.py:65
  338.5 205.5 %reduce-scatter.11.cloned.1.call-start = ((), (), s32[]{:S(2)}) async-start(), calls=%async_computation.12 | async-start | bytes 3538944 | tf_op jit(solution)/shard_map/reduce_scatter | solution.py:92
  397.5 44.6 %copy-start.2 = (bf16[768,2048]{1,0:T(8,128)(2,1)S(1)}, bf16[768,2048]{1,0:T(8,128)(2,1)}, u32[]{:S(2)}) copy-start(bf16[768,2048]{1,0:T(8,128)(2,1)} %all-gather.6.cloned.1.call-done) | copy-start | bytes 9437188
  441.1 180.4 %reduce-scatter.7.cloned.1.call-start = ((), (), s32[]{:S(2)}) async-start(), calls=%async_computation.7 | async-start | bytes 3538944 | tf_op jit(solution)/shard_map/reduce_scatter | solution.py:67
  445.2 40.5 %copy-start.6 = (f32[2048]{0:T(1024)S(1)}, f32[2048]{0:T(1024)}, u32[]{:S(2)}) copy-start(f32[2048]{0:T(1024)} %param.10) | copy-start | bytes 24580
  523.1 98.4 %copy-start.3 = (bf16[96,2048]{1,0:T(8,128)(2,1)S(1)}, bf16[96,2048]{1,0:T(8,128)(2,1)}, u32[]{:S(2)}) copy-start(bf16[96,2048]{1,0:T(8,128)(2,1)} %param.9) | copy-start | bytes 1179652
  523.1 100.2 %copy-start.4 = (bf16[96,2048]{1,0:T(8,128)(2,1)S(1)}, bf16[96,2048]{1,0:T(8,128)(2,1)}, u32[]{:S(2)}) copy-start(bf16[96,2048]{1,0:T(8,128)(2,1)} %param.17) | copy-start | bytes 1179652
Sparse Core Ops, SparseCore 0:
  10.2 62.7 all-gather.5
  75.1 58.7 all-gather.9
  188.7 87.8 reduce-scatter.4
  279.1 53.0 reduce-scatter.8
  337.3 41.8 all-gather.11
  380.6 41.8 all-gather.13
  424.1 41.8 all-gather.7
  469.6 74.3 reduce-scatter.10
  547.6 73.8 reduce-scatter.6
where the time goes:
time: 644 us; the launch traced here: 632 us
  waiting for transfers between devices  201 us (31%)
  matrix products  165 us (26%)
  local copies, waits for them, and re-layouts  150 us (23%)
  other arithmetic  65.4 us (10%)
  blocking collectives  36.3 us (6%)
  between operations  14.2 us (2%)
    mul x6, local copies, waits for them, and re-layouts, expand_mask(): weight.reshape(mask_rows, BLOCK, mask_cols, BLOCK)  148 us
    dot_general x3, matrix products, contract_rows(): lax.dot_general(left, right, (((0,), (0,)), ((), ())), preferred_element_...  57.6 us
    dot_general x3, matrix products, contract_cols(): lax.dot_general(left, right, (((1,), (1,)), ((), ())), preferred_element_...  56.6 us
    reduce_scatter x1, waiting for transfers between devices, shards(): lax.psum_scatter(contract_cols(row_block, down_eff).astype(jnp.bfloat16),...  50.6 us
    reduce_scatter x1, waiting for transfers between devices, shards(): lax.psum_scatter(jnp.dot(row_block, down_eff, preferred_element_type=jnp....  47.9 us
    all_gather x1, waiting for transfers between devices, shards(): lax.all_gather(d_gate, 'col', axis=0, tiled=True)  40.7 us
    mul x2, other arithmetic, expand_mask(): weight.reshape(mask_rows, BLOCK, mask_cols, BLOCK)  33.3 us
    all_gather x1, waiting for transfers between devices, shards(): lax.all_gather(d_up, 'col', axis=0, tiled=True)  25.1 us
  transfers between devices with their start and end apart: 9, of which 7 were waited for; matrix products, arithmetic and copies ran while one was open for 58% of the time, Pallas kernels for 0%

commit v1 on v0

--- a/solution.py
+++ b/solution.py
@@ -83,8 +83,27 @@
     d_gate = (
         d_hidden * up_value * sigmoid_gate * (1.0 + gate_value * (1.0 - sigmoid_gate))
     ).astype(jnp.bfloat16)
+
+    def recast_zones(my_data, shard_axis):
+        answer, new, ready = (
+            lax.psum(1, axis_name=shard_axis),
+            lax.axis_index(shard_axis),
+            my_data.shape[0],
+        )
+        entries = []
+        for dev in range(answer):
+            entries.append((dev, (dev + 1) % answer))
+        u_next = jnp.zeros((*my_data.shape[:0], answer * ready, *my_data.shape[1:]), my_data.dtype)
+        taken_in = my_data
+        for ix in range(answer):
+            res = (new - ix) % answer
+            u_next = lax.dynamic_update_slice_in_dim(u_next, taken_in, res * ready, axis=0)
+            if ix < answer - 1:
+                taken_in = lax.ppermute(taken_in, axis_name=shard_axis, perm=entries)
+        return u_next
+
     d_gate_all, d_up_all = (
-        lax.all_gather(d_gate, "col", axis=0, tiled=True),
+        recast_zones(d_gate, shard_axis="col"),
         lax.all_gather(d_up, "col", axis=0, tiled=True),
     )
     grad_w_gate = expand_mask(contract_rows(hidden_in, d_gate_all).astype(jnp.bfloat16), mask_gate)

time: 644 us -> 650 us (level)
  local copies, waits for them, and re-layouts: 150 us -> 160 us
  waiting for transfers between devices: 201 us -> 193 us
    ppermute x0 -> x3, waiting for transfers between devices: none -> 88.5 us  [recast_zones(): taken_in = lax.ppermute(taken_in, axis_name=shard_axis, perm=entries)]
    all_gather x1 -> x0, waiting for transfers between devices: 40.7 us -> none  [shards(): lax.all_gather(d_gate, 'col', axis=0, tiled=True)]
    all_gather x1, waiting for transfers between devices: 25.1 us -> 0.01 us  [shards(): lax.all_gather(d_up, 'col', axis=0, tiled=True)]
    all_gather x1, waiting for transfers between devices: 20.8 us -> 0.01 us  [shards(): hidden_all = lax.all_gather(hidden, 'col', axis=0, tiled=True)]
    reduce_scatter x1, waiting for transfers between devices: 47.9 us -> 40.1 us  [shards(): lax.psum_scatter(jnp.dot(row_block, down_eff, preferred_element_type=jnp....]
  transfers between devices with their start and end apart: 9 -> 11, of which waited for: 7 -> 6; matrix products, arithmetic and copies ran while one was open for 58% -> 59% of each run, Pallas kernels for 0% -> 0%
where the time goes in v1:
time: 650 us; the launch traced here: 639 us
  waiting for transfers between devices  193 us (30%)
  matrix products  165 us (25%)
  local copies, waits for them, and re-layouts  160 us (25%)
  other arithmetic  67.2 us (10%)
  blocking collectives  37 us (6%)
  between operations  14.8 us (2%)
    mul x6, local copies, waits for them, and re-layouts, expand_mask(): weight.reshape(mask_rows, BLOCK, mask_cols, BLOCK)  148 us
    ppermute x3, waiting for transfers between devices, recast_zones(): taken_in = lax.ppermute(taken_in, axis_name=shard_axis, perm=entries)  88.5 us
    dot_general x3, matrix products, contract_rows(): lax.dot_general(left, right, (((0,), (0,)), ((), ())), preferred_element_...  57.6 us
    dot_general x3, matrix products, contract_cols(): lax.dot_general(left, right, (((1,), (1,)), ((), ())), preferred_element_...  56.7 us
    reduce_scatter x1, waiting for transfers between devices, shards(): lax.psum_scatter(contract_cols(row_block, down_eff).astype(jnp.bfloat16),...  50.7 us
    reduce_scatter x1, waiting for transfers between devices, shards(): lax.psum_scatter(jnp.dot(row_block, down_eff, preferred_element_type=jnp....  40.1 us
    mul x2, other arithmetic, expand_mask(): weight.reshape(mask_rows, BLOCK, mask_cols, BLOCK)  33.3 us
    psum x1, blocking collectives, shards(): grad_gain = lax.psum(gain_part, 'row')  23.2 us
  transfers between devices with their start and end apart: 11, of which 6 were waited for; matrix products, arithmetic and copies ran while one was open for 59% of the time, Pallas kernels for 0%

profile of v1, /device:TPU:0, one launch (start us, length us, event | category | flops | bytes accessed | tf_op | source)
XLA Modules:
  0.0 638.6 jit_solution(18122712579947246461)
XLA Ops:
  7.2 0.0 all-gather.5.cloned.1.call-start
  7.2 0.7 all-gather.5.cloned.1.call-update
  7.9 0.0 all-gather.9.cloned.1.call-start
  7.9 0.7 all-gather.9.cloned.1.call-update
  8.6 0.0 reduce-scatter.5.cloned.1.call-start
  8.7 0.7 convert_element_type.77
  9.4 10.0 %mul.154 = bf16[32,64,56,64]{3,2,1,0:T(8,128)(2,1)} broadcast(bf16[32,56]{1,0:T(8,128)(2,1)S(1)} %convert_element_type.77), dimensions={0,2} | broadcast | bytes 14683648 | tf_op jit(solution)/shard_map/mul | solution.py:14
  19.4 36.2 %mul.155 = bf16[2048,3584]{1,0:T(8,128)(2,1)} reshape(bf16[32,64,56,64]{3,2,1,0:T(8,128)(2,1)} %mul.154) | data formatting | bytes 29360128 | tf_op jit(solution)/shard_map/mul | solution.py:14
  55.7 10.2 %mul.151 = bf16[32,64,56,64]{3,2,1,0:T(8,128)(2,1)} broadcast(bf16[32,56]{1,0:T(8,128)(2,1)S(1)} %convert_element_type.76), dimensions={0,2} | broadcast | bytes 14683648 | tf_op jit(solution)/shard_map/mul | solution.py:14
  65.8 36.2 %mul.152 = bf16[2048,3584]{1,0:T(8,128)(2,1)} reshape(bf16[32,64,56,64]{3,2,1,0:T(8,128)(2,1)} %mul.151) | data formatting | bytes 29360128 | tf_op jit(solution)/shard_map/mul | solution.py:14
  102.1 18.6 %mul.156 = bf16[2048,3584]{1,0:T(8,128)(2,1)} multiply(bf16[2048,3584]{1,0:T(8,128)(2,1)} %param.12, bf16[2048,3584]{1,0:T(8,128)(2,1)} %mul.155) | non-fusion elementwise | flops 7340032 | bytes 44040192 | tf_op jit(solution)/shard_map/mul | solution.py:14
  120.7 1.1 copy-done
  121.8 14.7 %mul.153 = bf16[2048,3584]{1,0:T(8,128)(2,1)} multiply(bf16[2048,3584]{1,0:T(8,128)(2,1)} %param.11, bf16[2048,3584]{1,0:T(8,128)(2,1)S(1)} %copy-done) | non-fusion elementwise | flops 7340032 | bytes 44040192 | tf_op jit(solution)/shard_map/mul | solution.py:14
  136.5 2.7 fusion.3
  139.3 8.1 %psum.21 = f32[768,1]{0,1:T(1,128)S(1)} all-reduce(f32[768,1]{0,1:T(1,128)S(1)} %broadcast_in_dim.6), channel_id=1, replica_groups=mesh['row'=8,'col'=4] {'col'}, use_global_device_ids=true, to_apply=%region_1.0 | all-reduce | flops 768 | bytes 6144 | tf_op jit(solution)/shard_map/psum | solution.py:43
  147.3 0.6 fusion.25
  147.9 17.5 %convolution_convert_fusion.4 = bf16[768,3584]{1,0:T(8,128)(2,1)} fusion(bf16[2048,3584]{1,0:T(8,128)(2,1)} %mul.156, f32[2048]{0:T(1024)S(1)} %copy-done.8, f32[768]{0:T(1024)S(1)} %get-tuple-element.10, bf16[768,2048]{1,0:T(8,128)(2,1)} %all-gather.5.cloned.1.call-done), kind=kOutput, calls=%fused_computation.10 | convolution fusion | flops 11283333120 | bytes 23342080 | tf_op jit(solution)/shard_map/dot_general | solution.py:52
  165.5 13.5 %convolution_convert_fusion.5 = bf16[768,3584]{1,0:T(8,128)(2,1)} fusion(bf16[2048,3584]{1,0:T(8,128)(2,1)S(1)} %bitcast.26, f32[2048]{0:T(1024)S(1)} %copy-done.8, f32[768]{0:T(1024)S(1)} %get-tuple-element.10, bf16[768,2048]{1,0:T(8,128)(2,1)S(1)} %copy-done.2), kind=kOutput, calls=%fused_computation.11 | convolution fusion | flops 11283333120 | bytes 23342080 | tf_op jit(solution)/shard_map/dot_general | solution.py:51
  179.0 9.5 %pad_maximum_fusion = bf16[768,7168]{1,0:T(8,128)(2,1)} fusion(bf16[768,3584]{1,0:T(8,128)(2,1)} %convolution_convert_fusion.4, bf16[768,3584]{1,0:T(8,128)(2,1)} %convolution_convert_fusion.5), kind=kLoop, calls=%fused_computation.6 | loop fusion | flops 22020096 | bytes 22020096 | tf_op jit(solution)/shard_map/concatenate | solution.py:49
  188.5 0.0 reduce-scatter.5.cloned.1.call-update
  188.5 0.2 reduce-scatter.9.cloned.1.call-start
  188.7 0.5 copy-done.11
  189.2 0.1 copy.15
  189.3 14.1 %mul.159 = bf16[56,64,32,64]{3,2,1,0:T(8,128)(2,1)} broadcast(bf16[56,32]{1,0:T(8,128)(2,1)S(1)} %copy.15), dimensions={0,2} | broadcast | bytes 14683648 | tf_op jit(solution)/shard_map/mul | solution.py:14
  203.4 40.8 %mul.160 = bf16[3584,2048]{1,0:T(8,128)(2,1)} reshape(bf16[56,64,32,64]{3,2,1,0:T(8,128)(2,1)} %mul.159) | data formatting | bytes 29360128 | tf_op jit(solution)/shard_map/mul | solution.py:14
  244.2 19.8 %fusion.4 = bf16[768,3584]{1,0:T(8,128)(2,1)} fusion(bf16[768,2048]{1,0:T(8,128)(2,1)} %all-gather.9.cloned.1.call-done, bf16[3584,2048]{1,0:T(8,128)(2,1)} %param.13, bf16[3584,2048]{1,0:T(8,128)(2,1)} %mul.160), kind=kOutput, calls=%fused_computation.15 | convolution fusion | flops 11284381696 | bytes 38010880 | tf_op jit(solution)/shard_map/dot_general | solution.py:27
  264.1 0.0 reduce-scatter.9.cloned.1.call-update
  264.1 0.0 all-gather.11.cloned.1.call-start
  264.1 12.4 %reduce-scatter.5.cloned.1.call-done = bf16[192,7168]{1,0:T(8,128)(2,1)} async-done(((bf16[768,7168]{1,0:T(8,128)(2,1)}), bf16[192,7168]{1,0:T(8,128)(2,1)}) %reduce-scatter.5.cloned.1.call-update) | async-done | bytes 2752528 | tf_op jit(solution)/shard_map/reduce_scatter | solution.py:48
  276.6 4.8 convert_element_type.78
  281.4 50.7 %reduce-scatter.9.cloned.1.call-done = bf16[192,3584]{1,0:T(8,128)(2,1)} async-done(((bf16[768,3584]{1,0:T(8,128)(2,1)}), bf16[192,3584]{1,0:T(8,128)(2,1)}) %reduce-scatter.9.cloned.1.call-update) | async-done | bytes 1376272 | tf_op jit(solution)/shard_map/reduce_scatter | solution.py:76
  332.0 5.5 fusion.14
  337.6 0.0 all-gather.11.cloned.1.call-update
  337.6 0.0 all-gather.7.cloned.1.call-start
  337.7 0.4 broadcast_in_dim.7
  338.0 0.9 copy-done.4
  338.9 1.7 copy-done.1
  340.6 1.2 constant_dynamic-update-slice_fusion.3
  341.8 2.4 copy-done.5
  344.2 44.6 %collective-permute-done = bf16[192,3584]{1,0:T(8,128)(2,1)S(1)} collective-permute-done((bf16[192,3584]{1,0:T(8,128)(2,1)S(1)}, bf16[192,3584]{1,0:T(8,128)(2,1)S(1)}, u32[]{:S(2)}, u32[]{:S(2)}) %collective-permute-start) | collective-permute-done | bytes 1376288 | tf_op jit(solution)/shard_map/ppermute | solution.py:102
  388.8 17.7 %collective-permute-done.1 = bf16[192,3584]{1,0:T(8,128)(2,1)S(1)} collective-permute-done((bf16[192,3584]{1,0:T(8,128)(2,1)S(1)}, bf16[192,3584]{1,0:T(8,128)(2,1)S(1)}, u32[]{:S(2)}, u32[]{:S(2)}) %collective-permute-start.1) | collective-permute-done | bytes 1376288 | tf_op jit(solution)/shard_map/ppermute | solution.py:102
  406.5 0.0 all-gather.7.cloned.1.call-update
  406.5 0.3 reduce-scatter.11.cloned.1.call-start
  406.8 1.2 constant_dynamic-update-slice_fusion.2
  408.0 1.2 constant_dynamic-update-slice_fusion.1
  409.2 26.2 %collective-permute-done.2 = bf16[192,3584]{1,0:T(8,128)(2,1)} collective-permute-done((bf16[192,3584]{1,0:T(8,128)(2,1)S(1)}, bf16[192,3584]{1,0:T(8,128)(2,1)}, u32[]{:S(2)}, u32[]{:S(2)}) %collective-permute-start.2) | collective-permute-done | bytes 1376288 | tf_op jit(solution)/shard_map/ppermute | solution.py:102
  435.4 2.5 constant_dynamic-update-slice_fusion
  437.9 18.2 %fusion.26 = f32[768,2048]{1,0:T(8,128)} fusion(bf16[768,3584]{1,0:T(8,128)(2,1)} %all-gather.11.cloned.1.call-done, bf16[2048,3584]{1,0:T(8,128)(2,1)} %mul.156), kind=kOutput, calls=%fused_computation.48 | convolution fusion | flops 11274289152 | bytes 26476544 | tf_op jit(solution)/shard_map/dot_general | solution.py:27
  456.1 18.7 %add_convert_fusion = bf16[768,2048]{1,0:T(8,128)(2,1)} fusion(f32[768,2048]{1,0:T(8,128)} %fusion.26, bf16[768,3584]{1,0:T(8,128)(2,1)} %constant_dynamic-update-slice_fusion, bf16[2048,3584]{1,0:T(8,128)(2,1)} %mul.153), kind=kOutput, calls=%fused_computation.13 | convolution fusion | flops 11277434880 | bytes 29622272 | tf_op jit(solution)/shard_map/dot_general | solution.py:27
  474.7 0.0 reduce-scatter.11.cloned.1.call-update
  474.8 0.3 reduce-scatter.7.cloned.1.call-start
  475.1 0.8 fusion.23
  475.8 3.1 convert_multiply_fusion
  479.0 20.0 %fusion.8 = bf16[768,2048]{1,0:T(8,128)(2,1)} fusion(bf16[768,3584]{1,0:T(8,128)(2,1)} %all-gather.7.cloned.1.call-done, bf16[3584,2048]{1,0:T(8,128)(2,1)} %param.13, bf16[3584,2048]{1,0:T(8,128)(2,1)} %mul.160), kind=kOutput, calls=%fused_computation.21 | convolution fusion | flops 11283202048 | bytes 38010880 | tf_op jit(solution)/shard_map/dot_general | solution.py:68
  499.0 0.0 reduce-scatter.7.cloned.1.call-update
  499.0 18.8 %fusion = bf16[2048,3584]{1,0:T(8,128)(2,1)} fusion(bf16[2048,3584]{1,0:T(8,128)(2,1)} %mul.152, bf16[768,3584]{1,0:T(8,128)(2,1)} %constant_dynamic-update-slice_fusion, f32[2048]{0:T(1024)S(1)} %copy-done.9, f32[768]{0:T(1024)S(1)} %get-tuple-element.10, bf16[768,2048]{1,0:T(8,128)(2,1)S(1)} %copy-done.3), kind=kOutput, calls=%fused_computation.3 | convolution fusion | flops 11295260672 | bytes 38022144 | tf_op jit(solution)/shard_map/dot_general | solution.py:21
  517.8 18.7 %fusion.1 = bf16[2048,3584]{1,0:T(8,128)(2,1)} fusion(bf16[2048,3584]{1,0:T(8,128)(2,1)} %mul.155, bf16[768,3584]{1,0:T(8,128)(2,1)} %all-gather.11.cloned.1.call-done, f32[2048]{0:T(1024)S(1)} %copy-done.9, f32[768]{0:T(1024)S(1)} %get-tuple-element.10, bf16[768,2048]{1,0:T(8,128)(2,1)S(1)} %copy-done.3), kind=kOutput, calls=%fused_computation.4 | convolution fusion | flops 11295260672 | bytes 38022144 | tf_op jit(solution)/shard_map/dot_general | solution.py:21
  536.4 20.2 %fusion.2 = bf16[3584,2048]{1,0:T(8,128)(2,1)} fusion(bf16[3584,2048]{1,0:T(8,128)(2,1)} %mul.160, bf16[768,3584]{1,0:T(8,128)(2,1)} %all-gather.7.cloned.1.call-done, bf16[768,2048]{1,0:T(8,128)(2,1)} %all-gather.9.cloned.1.call-done), kind=kOutput, calls=%fused_computation.5 | convolution fusion | flops 11288969216 | bytes 38010880 | tf_op jit(solution)/shard_map/dot_general | solution.py:21
  556.6 1.5 fusion.22
  558.1 5.7 psum.22
  563.8 23.2 %psum.23 = f32[2048]{0:T(1024)} all-reduce(f32[2048]{0:T(1024)S(1)} %get-tuple-element.6), channel_id=1, replica_groups=mesh['row'=8,'col'=4] {'row'}, use_global_device_ids=true, to_apply=%region_9.10 | all-reduce | flops 2048 | bytes 16384 | tf_op jit(solution)/shard_map/psum | solution.py:126
  587.0 40.1 %reduce-scatter.7.cloned.1.call-done = bf16[96,2048]{1,0:T(8,128)(2,1)} async-done(((bf16[768,2048]{1,0:T(8,128)(2,1)}), bf16[96,2048]{1,0:T(8,128)(2,1)}) %reduce-scatter.7.cloned.1.call-update) | async-done | bytes 393232 | tf_op jit(solution)/shard_map/reduce_scatter | solution.py:67
  627.2 1.8 add_convert_fusion.1
  629.0 2.3 fusion.21
  (40 shorter events, 0.1 us)
Async XLA Ops:
  7.2 129.4 %all-gather.5.cloned.1.call-start = ((), (), s32[]{:S(2)}) async-start(), calls=%async_computation.4 | async-start | bytes 3538944 | tf_op jit(solution)/shard_map/all_gather | solution.py:38
  7.9 236.3 %all-gather.9.cloned.1.call-start = ((), (), s32[]{:S(2)}) async-start(), calls=%async_computation.8 | async-start | bytes 3538944 | tf_op jit(solution)/shard_map/all_gather | solution.py:39
  8.6 267.9 %reduce-scatter.5.cloned.1.call-start = ((), (), s32[]{:S(2)}) async-start(), calls=%async_computation.5 | async-start | bytes 13762560 | tf_op jit(solution)/shard_map/reduce_scatter | solution.py:48
  19.4 36.2 %copy-start.10 = (s32[32,56]{1,0:T(8,128)S(1)}, s32[32,56]{1,0:T(8,128)}, u32[]{:S(2)}) copy-start(s32[32,56]{1,0:T(8,128)} %param.14) | copy-start | bytes 21508
  102.1 19.7 %copy-start = (bf16[2048,3584]{1,0:T(8,128)(2,1)S(1)}, bf16[2048,3584]{1,0:T(8,128)(2,1)}, u32[]{:S(2)}) copy-start(bf16[2048,3584]{1,0:T(8,128)(2,1)} %mul.152) | copy-start | bytes 44040196
  121.8 26.1 %copy-start.8 = (f32[2048]{0:T(1024)S(1)}, f32[2048]{0:T(1024)}, u32[]{:S(2)}) copy-start(f32[2048]{0:T(1024)} %param.10) | copy-start | bytes 24580
  136.5 28.9 %slice-start = ((s8[14680064]{0:T(1024)(128)(4,1)}), s8[2097152]{0:T(1024)(128)(4,1)S(1)}, s32[]{:S(2)}) async-start(s8[14680064]{0:T(1024)(128)(4,1)} %bitcast.25), calls=%async_computation.12 | async-start | bytes 4194304
  147.9 17.5 %slice-start.1 = ((s8[14680064]{0:T(1024)(128)(4,1)}), s8[4194304]{0:T(1024)(128)(4,1)S(1)}, s32[]{:S(2)}) async-start(s8[14680064]{0:T(1024)(128)(4,1)} %bitcast.25), calls=%async_computation.13 | async-start | bytes 8388608
  147.9 17.5 %slice-start.2 = ((s8[14680064]{0:T(1024)(128)(4,1)}), s8[4194304]{0:T(1024)(128)(4,1)S(1)}, s32[]{:S(2)}) async-start(s8[14680064]{0:T(1024)(128)(4,1)} %bitcast.25), calls=%async_computation.14 | async-start | bytes 8388608
  147.9 17.5 %slice-start.3 = ((s8[14680064]{0:T(1024)(128)(4,1)}), s8[4194304]{0:T(1024)(128)(4,1)S(1)}, s32[]{:S(2)}) async-start(s8[14680064]{0:T(1024)(128)(4,1)} %bitcast.25), calls=%async_computation.15 | async-start | bytes 8388608
  147.9 17.5 %copy-start.2 = (bf16[768,2048]{1,0:T(8,128)(2,1)S(1)}, bf16[768,2048]{1,0:T(8,128)(2,1)}, u32[]{:S(2)}) copy-start(bf16[768,2048]{1,0:T(8,128)(2,1)} %all-gather.5.cloned.1.call-done) | copy-start | bytes 9437188
  188.5 0.7 copy-start.11
  188.5 143.5 %reduce-scatter.9.cloned.1.call-start = ((), (), s32[]{:S(2)}) async-start(), calls=%async_computation.9 | async-start | bytes 6881280 | tf_op jit(solution)/shard_map/reduce_scatter | solution.py:76
  264.1 173.8 %all-gather.11.cloned.1.call-start = ((), (), s32[]{:S(2)}) async-start(), calls=%async_computation.10 | async-start | bytes 6881280 | tf_op jit(solution)/shard_map/all_gather | solution.py:107
  337.5 1.3 copy-start.4
  337.6 141.4 %all-gather.7.cloned.1.call-start = ((), (), s32[]{:S(2)}) async-start(), calls=%async_computation.6 | async-start | bytes 6881280 | tf_op jit(solution)/shard_map/all_gather | solution.py:65
  337.6 2.9 copy-start.1
  341.8 2.4 copy-start.5
  344.2 44.6 %collective-permute-start = (bf16[192,3584]{1,0:T(8,128)(2,1)S(1)}, bf16[192,3584]{1,0:T(8,128)(2,1)S(1)}, u32[]{:S(2)}, u32[]{:S(2)}) collective-permute-start(bf16[192,3584]{1,0:T(8,128)(2,1)S(1)} %get-tuple-element.9), channel_id=1, source_target_pairs={{0,1},{1,2},{2,3},{3,0},{4,5},{5,6},{6,7},{7,4},{8,9},{9,10},{10,1... | collective-permute-start | bytes 4128776 | tf_op jit(solution)/shard_map/ppermute | solution.py:102
  388.8 17.7 %collective-permute-start.1 = (bf16[192,3584]{1,0:T(8,128)(2,1)S(1)}, bf16[192,3584]{1,0:T(8,128)(2,1)S(1)}, u32[]{:S(2)}, u32[]{:S(2)}) collective-permute-start(bf16[192,3584]{1,0:T(8,128)(2,1)S(1)} %collective-permute-done), channel_id=1, source_target_pairs={{0,1},{1,2},{2,3},{3,0},{4,5},{5,6},{6,7},{7,4},{8,9},{9,10},{10,1... | collective-permute-start | bytes 4128776 | tf_op jit(solution)/shard_map/ppermute | solution.py:102
  406.5 28.8 %collective-permute-start.2 = (bf16[192,3584]{1,0:T(8,128)(2,1)S(1)}, bf16[192,3584]{1,0:T(8,128)(2,1)}, u32[]{:S(2)}, u32[]{:S(2)}) collective-permute-start(bf16[192,3584]{1,0:T(8,128)(2,1)S(1)} %collective-permute-done.1), channel_id=1, source_target_pairs={{0,1},{1,2},{2,3},{3,0},{4,5},{5,6},{6,7},{7,4},{8,9},{9,10},{10,1... | collective-permute-start | bytes 4128776 | tf_op jit(solution)/shard_map/ppermute | solution.py:102
  406.5 150.1 %reduce-scatter.11.cloned.1.call-start = ((), (), s32[]{:S(2)}) async-start(), calls=%async_computation.11 | async-start | bytes 3538944 | tf_op jit(solution)/shard_map/reduce_scatter | solution.py:111
  456.1 19.8 %copy-start.3 = (bf16[768,2048]{1,0:T(8,128)(2,1)S(1)}, bf16[768,2048]{1,0:T(8,128)(2,1)}, u32[]{:S(2)}) copy-start(bf16[768,2048]{1,0:T(8,128)(2,1)} %all-gather.5.cloned.1.call-done) | copy-start | bytes 9437188
  474.8 152.4 %reduce-scatter.7.cloned.1.call-start = ((), (), s32[]{:S(2)}) async-start(), calls=%async_computation.7 | async-start | bytes 3538944 | tf_op jit(solution)/shard_map/reduce_scatter | solution.py:67
  479.0 20.0 %copy-start.9 = (f32[2048]{0:T(1024)S(1)}, f32[2048]{0:T(1024)}, u32[]{:S(2)}) copy-start(f32[2048]{0:T(1024)} %param.10) | copy-start | bytes 24580
  536.4 90.7 %copy-start.6 = (bf16[96,2048]{1,0:T(8,128)(2,1)S(1)}, bf16[96,2048]{1,0:T(8,128)(2,1)}, u32[]{:S(2)}) copy-start(bf16[96,2048]{1,0:T(8,128)(2,1)} %param.9) | copy-start | bytes 1179652
  536.4 92.6 %copy-start.7 = (bf16[96,2048]{1,0:T(8,128)(2,1)S(1)}, bf16[96,2048]{1,0:T(8,128)(2,1)}, u32[]{:S(2)}) copy-start(bf16[96,2048]{1,0:T(8,128)(2,1)} %param.17) | copy-start | bytes 1179652
Sparse Core Ops, SparseCore 0:
  10.2 62.7 all-gather.4
  75.1 58.6 all-gather.8
  188.6 87.9 reduce-scatter.4
  279.0 53.0 reduce-scatter.8
  337.7 55.3 all-gather.10
  406.7 48.6 all-gather.6
  474.9 74.4 reduce-scatter.10
  553.0 74.1 reduce-scatter.6
